TPU v7x, 256 devices: a whole 4x4x8 slice. The times are simulated.
256 devices in a mesh: ctx: 128 (over x, y, z), head: 2 (over core).
Axes of the slice: x: 4, y: 4, z: 8, core: 2. Of those that a mesh axis runs over, the one named last changes fastest.
Arguments:
- queries: bfloat16 [16384, 3072], P('ctx', 'head'), may hold values from -6 to 6
- keys: bfloat16 [16384, 3072], P('ctx', 'head'), may hold values from -6 to 6
- values: bfloat16 [16384, 3072], P('ctx', 'head'), may hold values from -30 to 30
- decay_log: float32 [32, 16384], P('head', 'ctx'), may hold values from -1 to 0
- norm_gain: float32 [3072], P('head'), may hold values from 0.25 to 1.75
- out_grad: bfloat16 [16384, 3072], P('ctx', 'head'), may hold values from -6 to 6
- doc_lengths: int32 [16], replicated, may hold values from 1 to 4096, 16384 in all
Outputs:
- attn_output: bfloat16 [16384, 3072], P('ctx', 'head')
- query_grad: bfloat16 [16384, 3072], P('ctx', 'head')
- key_grad: bfloat16 [16384, 3072], P('ctx', 'head')
- value_grad: bfloat16 [16384, 3072], P('ctx', 'head')
Inputs may be any that keep to these rules, and one draw needn't show every extreme that they name: `doc_lengths`: the 16 lengths sum to 16384; the longest is exactly 4096.
All inputs are finite; a program needn't handle non-finite values.
Results may differ from a plain program's by a relative error of at most 0.01.
Values sent between devices are 32-bit elements; how exact they have to be, the bound alone decides.
A program may use at most 256 MiB of HBM per device.

v0:
```python
import math

import jax
import jax.numpy as jnp
from jax import lax
from jax.sharding import PartitionSpec as P

EPSILON = 1e-06


def entering(part, axis, combine, identity, reverse):
    count = lax.axis_size(axis)
    place = lax.axis_index(axis)
    ahead = count - 1 - place if reverse else place
    gathered = jax.tree.map(lambda a: lax.all_gather(a, axis), part)
    state = jax.tree.map(lambda a, e: jnp.zeros_like(a) + jnp.asarray(e, a.dtype), part, identity)

    def one(hop, state):
        source = count - 1 - hop if reverse else hop
        return combine(
            state, jax.tree.map(lambda a: lax.dynamic_index_in_dim(a, source, 0, False), gathered)
        )

    return lax.fori_loop(0, ahead, one, state)


def doc_starts(doc_lengths):
    doc_ends = jnp.cumsum(doc_lengths)
    return doc_ends - doc_lengths


def geometry(decay_block, block_start, starts_doc):
    row_count = decay_block.shape[1]
    positions = block_start + jnp.arange(row_count, dtype=jnp.int32)
    doc_index = jnp.sum((starts_doc[None, :] <= positions[:, None]).astype(jnp.int32), axis=1)
    doc_before = jnp.sum((starts_doc <= block_start - 1).astype(jnp.int32))
    carry_mask = (doc_index == doc_before).astype(decay_block.dtype)
    log_cum = jnp.cumsum(decay_block, axis=1)
    causal = positions[:, None] >= positions[None, :]
    same_doc = jnp.logical_and(causal, doc_index[:, None] == doc_index[None, :])
    log_gap = jnp.where(same_doc[None], log_cum[:, :, None] - log_cum[:, None, :], 0.0)
    decay_mask = jnp.exp(log_gap) * same_doc[None].astype(decay_block.dtype)
    keep_last = (doc_index == doc_index[row_count - 1]).astype(decay_block.dtype)
    exit_weight = jnp.exp(log_cum[:, row_count - 1 : row_count] - log_cum) * keep_last[None, :]
    reach_in = carry_mask[None, :] * jnp.exp(log_cum)
    factor = reach_in[:, row_count - 1]
    return (decay_mask, exit_weight, reach_in, factor)


def combine(earlier, later_pair):
    return (earlier[0] * later_pair[0], later_pair[0][:, None, None] * earlier[1] + later_pair[1])


def split_pair(array):
    high = array.astype(jnp.bfloat16)
    low = (array - high.astype(jnp.float32)).astype(jnp.bfloat16)
    return (high, low)


def pair_einsum(form, first, second):
    if first.dtype == jnp.float32:
        high, low = split_pair(first)
        return jnp.einsum(form, high, second, preferred_element_type=jnp.float32) + jnp.einsum(
            form, low, second, preferred_element_type=jnp.float32
        )
    high, low = split_pair(second)
    return jnp.einsum(form, first, high, preferred_element_type=jnp.float32) + jnp.einsum(
        form, first, low, preferred_element_type=jnp.float32
    )


def on_device(queries, keys, values, decay_log, norm_gain, out_grad, doc_lengths):
    row_count, local_width = queries.shape
    head_count = decay_log.shape[0]
    head_width = local_width // head_count
    score_scale = 1.0 / math.sqrt(head_width)
    feature_count = local_width * lax.axis_size("head")
    block_start = lax.axis_index("ctx") * row_count
    starts_doc = doc_starts(doc_lengths)
    decay_mask, exit_weight, reach_in, factor = geometry(decay_log, block_start, starts_doc)
    query_heads = queries.reshape(row_count, head_count, head_width)
    key_heads = keys.reshape(row_count, head_count, head_width)
    value_heads = values.reshape(row_count, head_count, head_width)
    weighted_keys = key_heads.astype(jnp.float32) * exit_weight.T[:, :, None]
    exit_local = pair_einsum("shd,she->hde", weighted_keys, value_heads)
    zero_state = jnp.zeros_like(exit_local)
    prefix_pair = entering(
        (factor, exit_local), "ctx", combine, (jnp.ones_like(factor), zero_state), False
    )
    incoming = prefix_pair[1]
    scores = jnp.einsum("thd,shd->hts", query_heads, key_heads, preferred_element_type=jnp.float32)
    attn_probs = (scores * score_scale * decay_mask).astype(jnp.bfloat16)
    local_part = jnp.einsum(
        "hts,shd->thd", attn_probs, value_heads, preferred_element_type=jnp.float32
    )
    carried = pair_einsum("thd,hde->the", query_heads, incoming)
    attended = (local_part + score_scale * reach_in.T[:, :, None] * carried).reshape(
        row_count, local_width
    )
    square_sum = lax.psum(jnp.sum(attended * attended, axis=1), "head")
    inv_rms = lax.rsqrt(square_sum / feature_count + EPSILON)
    attn_output = (attended * inv_rms[:, None] * norm_gain[None, :]).astype(jnp.bfloat16)
    grad_gain = out_grad.astype(jnp.float32) * norm_gain[None, :]
    grad_dot = lax.psum(jnp.sum(grad_gain * attended, axis=1), "head")
    attended_grad = (
        grad_gain * inv_rms[:, None] - attended * (inv_rms**3 * grad_dot / feature_count)[:, None]
    ).astype(jnp.bfloat16)
    grad_heads = attended_grad.reshape(row_count, head_count, head_width)
    reached_queries = query_heads.astype(jnp.float32) * reach_in.T[:, :, None]
    block_grad = score_scale * pair_einsum("thd,the->hde", reached_queries, grad_heads)
    suffix_pair = entering(
        (factor, block_grad), "ctx", combine, (jnp.ones_like(factor), zero_state), True
    )
    later_state = suffix_pair[1]
    grad_scores = jnp.einsum(
        "thd,shd->hts", grad_heads, value_heads, preferred_element_type=jnp.float32
    )
    score_grad = (grad_scores * score_scale * decay_mask).astype(jnp.bfloat16)
    query_part = jnp.einsum(
        "hts,shd->thd", score_grad, key_heads, preferred_element_type=jnp.float32
    )
    query_part = query_part + score_scale * reach_in.T[:, :, None] * pair_einsum(
        "the,hde->thd", grad_heads, incoming
    )
    key_part = jnp.einsum(
        "hts,thd->shd", score_grad, query_heads, preferred_element_type=jnp.float32
    )
    key_part = key_part + exit_weight.T[:, :, None] * pair_einsum(
        "she,hde->shd", value_heads, later_state
    )
    value_part = jnp.einsum(
        "hts,the->she", attn_probs, grad_heads, preferred_element_type=jnp.float32
    )
    value_part = value_part + exit_weight.T[:, :, None] * pair_einsum(
        "shd,hde->she", key_heads, later_state
    )
    query_grad = query_part.reshape(row_count, local_width).astype(jnp.bfloat16)
    key_grad = key_part.reshape(row_count, local_width).astype(jnp.bfloat16)
    value_grad = value_part.reshape(row_count, local_width).astype(jnp.bfloat16)
    return (attn_output, query_grad, key_grad, value_grad)


def solution(mesh):
    in_specs = (
        P("ctx", "head"),
        P("ctx", "head"),
        P("ctx", "head"),
        P("head", "ctx"),
        P("head"),
        P("ctx", "head"),
        P(),
    )
    out_specs = (P("ctx", "head"), P("ctx", "head"), P("ctx", "head"), P("ctx", "head"))
    return jax.shard_map(
        on_device, mesh=mesh, in_specs=in_specs, out_specs=out_specs, check_vma=False
    )
```

profile of v0, /device:TPU:1, one launch (start us, length us, event | category | flops | bytes accessed | tf_op | source)
XLA Modules:
  0.0 1419.9 jit_solution(14331651619184359977)
XLA Ops:
  19.2 316.8 %all-reduce = f32[2048]{0:T(1024)S(1)} all-reduce(f32[2048]{0:T(1024)S(1)} %dynamic-update-slice), channel_id=2, replica_groups=mesh['ctx'=128,'head'=2] {'ctx'}, use_global_device_ids=true, to_apply=%add | all-reduce | flops 2048 | bytes 16384
  338.7 1.4 fusion.2
  340.1 159.8 %all-gather.6.cloned.1.call-done = f32[2048,96,96]{2,1,0:T(8,128)} async-done(((f32[16,96,96]{2,1,0:T(8,128)}), f32[2048,96,96]{2,1,0:T(8,128)}) %all-gather.6.cloned.1.call-update) | async-done | bytes 75497488 | tf_op jit(solution)/shard_map/all_gather | solution.py:15
  500.7 1.5 multiply_reduce_fusion
  503.2 3.1 all-reduce.1
  506.3 1.8 fusion.24
  508.5 1.3 fusion.14
  509.8 1.4 fusion.3
  513.9 1.9 copy.75
  515.8 633.6 %all-gather.8.cloned.1.call-done = f32[2048,96,96]{2,1,0:T(8,128)} async-done(((f32[16,96,96]{2,1,0:T(8,128)}), f32[2048,96,96]{2,1,0:T(8,128)}) %all-gather.8.cloned.1.call-update) | async-done | bytes 75497488 | tf_op jit(solution)/shard_map/all_gather | solution.py:15
  1149.5 257.9 %while.27 = (s32[]{:T(128)}, f32[16,96,96]{2,1,0:T(8,128)S(1)}, s32[]{:T(128)}, f32[128,16]{1,0:T(8,128)}, f32[128,16,96,96]{3,2,1,0:T(8,128)}, /*index=5*/s32[]{:T(128)}, s32[]{:T(128)}, s32[]{:T(128)}, s32[]{:T(128)}) while((s32[]{:T(128)}, f32[16,96,96]{2,1,0:T(8,128)S(1)}, s32[]{:T(128)}, f32[128,16]{1,0:T(8,128)}, ...), condition=%wide.region_11.12_spmd, body=%wide.region_10.11_spmd.sunk | while | flops 294918 | bytes 1769811 | solution.py:24
  1150.2 1.3 bitcast_add_fusion.5
  1152.2 1.3 bitcast_add_fusion.5
  1154.3 1.3 bitcast_add_fusion.5
  1156.3 1.3 bitcast_add_fusion.5
  1158.3 1.3 bitcast_add_fusion.5
  1160.4 1.3 bitcast_add_fusion.5
  1162.4 1.3 bitcast_add_fusion.5
  1164.4 1.3 bitcast_add_fusion.5
  1166.4 1.3 bitcast_add_fusion.5
  1168.5 1.3 bitcast_add_fusion.5
  1170.5 1.3 bitcast_add_fusion.5
  1172.5 1.3 bitcast_add_fusion.5
  1174.6 1.3 bitcast_add_fusion.5
  1176.6 1.3 bitcast_add_fusion.5
  1178.6 1.3 bitcast_add_fusion.5
  1180.7 1.3 bitcast_add_fusion.5
  1182.7 1.3 bitcast_add_fusion.5
  1184.7 1.3 bitcast_add_fusion.5
  1186.7 1.3 bitcast_add_fusion.5
  1188.8 1.3 bitcast_add_fusion.5
  1190.8 1.3 bitcast_add_fusion.5
  1192.8 1.3 bitcast_add_fusion.5
  1194.8 1.3 bitcast_add_fusion.5
  1196.9 1.3 bitcast_add_fusion.5
  1198.9 1.3 bitcast_add_fusion.5
  1201.0 1.3 bitcast_add_fusion.5
  1203.0 1.3 bitcast_add_fusion.5
  1205.0 1.3 bitcast_add_fusion.5
  1207.1 1.3 bitcast_add_fusion.5
  1209.1 1.3 bitcast_add_fusion.5
  1211.1 1.3 bitcast_add_fusion.5
  1213.2 1.3 bitcast_add_fusion.5
  1215.2 1.3 bitcast_add_fusion.5
  1217.2 1.3 bitcast_add_fusion.5
  1219.3 1.3 bitcast_add_fusion.5
  1408.3 1.3 fusion.18
  1410.8 1.3 fusion.17
  (277 shorter events, 229.6 us)
Async XLA Ops:
  7.2 492.8 %all-gather.6.cloned.1.call-start = ((), (), s32[]{:S(2)}) async-start(), calls=%async_computation | async-start | bytes 101449728 | tf_op jit(solution)/shard_map/all_gather | solution.py:15
  11.1 495.2 %copy-start.1 = (f32[16,128]{1,0:T(8,128)}, f32[16,128]{1,0:T(8,128)S(1)}, u32[]{:S(2)}) copy-start(f32[16,128]{1,0:T(8,128)S(1)} %reduce_window_sum.18) | copy-start | bytes 24580
  16.8 1132.7 %all-gather.8.cloned.1.call-start = ((), (), s32[]{:S(2)}) async-start(), calls=%async_computation.1 | async-start | bytes 101449728 | tf_op jit(solution)/shard_map/all_gather | solution.py:15
  18.8 487.5 %copy-start.2 = (f32[128,16]{0,1:T(8,128)}, f32[128,16]{0,1:T(8,128)S(1)}, u32[]{:S(2)}) copy-start(f32[128,16]{0,1:T(8,128)S(1)} %get-tuple-element.172) | copy-start | bytes 24580
  338.7 167.6 %copy-start.4 = (f32[128,128]{1,0:T(8,128)}, f32[128,128]{1,0:T(8,128)S(1)}, u32[]{:S(2)}) copy-start(f32[128,128]{1,0:T(8,128)S(1)} %get-tuple-element.179) | copy-start | bytes 196612
  338.7 167.6 %copy-start.5 = (pred[128,128]{1,0:T(8,128)(4,1)}, pred[128,128]{1,0:T(8,128)(4,1)S(1)}, u32[]{:S(2)}) copy-start(pred[128,128]{1,0:T(8,128)(4,1)S(1)} %get-tuple-element.178) | copy-start | bytes 49156
  500.0 6.3 copy-start.3
  511.3 1.7 copy-start
Sparse Core Ops, SparseCore 0:
  16.9 482.9 all-gather.5
  510.0 639.4 all-gather.7
where the time goes:
time: 1430 us; the launch traced here: 1420 us
  waiting for transfers between devices  793 us (55%)
  blocking collectives  320 us (22%)
  other arithmetic  173 us (12%)
  local copies, waits for them, and re-layouts  100 us (7%)
  between operations  15 us (1%)
    all_gather x2, waiting for transfers between devices, entering(): gathered = jax.tree.map(lambda a: lax.all_gather(a, axis), part)  793 us
    unnamed x1, blocking collectives  317 us
    add x127, other arithmetic, combine(): later_pair[0][:, None, None] * earlier[1] + later_pair[1]  166 us
    mul x127, local copies, waits for them, and re-layouts, combine(): later_pair[0][:, None, None] * earlier[1] + later_pair[1]  87.3 us
  transfers between devices with their start and end apart: 2, of which 2 were waited for; matrix products, arithmetic and copies ran while one was open for 1% of the time, Pallas kernels for 0%

commit v1 on v0

v1 whole, which is shorter than its diff:
```python
import functools
import math

import jax
import jax.numpy as jnp
from jax import lax
from jax.experimental import pallas as pl
from jax.experimental.pallas import tpu as pltpu
from jax.sharding import PartitionSpec as P

EPSILON = 1e-06
MESH = pl.DeviceIdType.MESH
F32 = jnp.float32
BF16 = jnp.bfloat16

RING = 8
REACH = 4
GROUP = 4
OFFSETS = (1, -1, 2, -2, 3, -3, 4)
PIECES = 2


def contract(a, b, ca, cb):
    return lax.dot_general(a, b, (((ca,), (cb,)), ((), ())), preferred_element_type=F32)


def split_pair(x):
    high = x.astype(BF16)
    return high, (x - high.astype(F32)).astype(BF16)


def kernel(
    head_dim,
    feature_count,
    lines,
    docs,
    q_ref,
    k_ref,
    v_ref,
    decay_ref,
    gain_ref,
    og_ref,
    o_ref,
    dq_ref,
    dk_ref,
    dv_ref,
    att,
    grad,
    crx,
    xw,
    cm,
    probs,
    kpart,
    vpart,
    send_a,
    recv_a,
    back_a,
    come_a,
    send_b,
    recv_b,
    back_b,
    come_b,
    tot_a,
    rtot_a,
    tot_b,
    rtot_b,
    fac,
    rfac,
    lfac,
    rlfac_a,
    rlfac_b,
    sums,
    rsums,
    there_s,
    there_r,
    line_s,
    line_r,
    back_s,
    back_r,
    fac_s,
    fac_r,
    lfac_s,
    lfac_r,
    sum_s,
    sum_r,
):
    rows = q_ref.shape[0]
    width = GROUP * head_dim
    groups = q_ref.shape[1] // width
    half = head_dim // 2
    scale = 1.0 / math.sqrt(head_dim)
    place = lax.axis_index("ctx")
    core = lax.axis_index("head")
    z = lax.rem(place, RING)
    line = lax.div(place, RING)

    def in_line(other):
        return (line * RING + other, core)

    def ring(offset):
        return lax.rem(z + (offset + RING), RING)

    def other_line(offset):
        return (lax.rem(line + (offset + lines), lines) * RING + z, core)

    barrier = pltpu.get_barrier_semaphore()
    partners = [in_line(ring(k)) for k in OFFSETS]
    partners += [other_line(s * k) for k in range(1, REACH + 1) for s in (1, -1)]
    partners += [(place, 1 - core)]
    for device in partners:
        pl.semaphore_signal(barrier, inc=1, device_id=device, device_id_type=MESH)

    start = place * rows
    col = start + lax.broadcasted_iota(jnp.int32, (rows, 1), 0)
    row = start + lax.broadcasted_iota(jnp.int32, (1, rows), 1)
    doc_col = jnp.zeros((rows, 1), jnp.int32)
    doc_row = jnp.zeros((1, rows), jnp.int32)
    before = jnp.int32(0)
    last = jnp.int32(0)
    begins = jnp.int32(0)
    for i in range(docs.shape[0]):
        doc_col += (begins <= col).astype(jnp.int32)
        doc_row += (begins <= row).astype(jnp.int32)
        before += (begins <= start - 1).astype(jnp.int32)
        last += (begins <= start + (rows - 1)).astype(jnp.int32)
        begins = begins + docs[i]
    carried_in = (doc_col == before).astype(F32)
    keep_last = (doc_col == last).astype(F32)
    same = jnp.logical_and(col >= row, doc_col == doc_row)

    decay = decay_ref[...]
    ti = lax.broadcasted_iota(jnp.int32, (rows, rows), 0)
    si = lax.broadcasted_iota(jnp.int32, (rows, rows), 1)
    lower = (si <= ti).astype(F32)
    log_col = lax.dot_general(
        lower, decay, (((1,), (1,)), ((), ())),
        precision=lax.Precision.HIGHEST, preferred_element_type=F32,
    )
    log_row = lax.dot_general(
        decay, lower, (((1,), (1,)), ((), ())),
        precision=lax.Precision.HIGHEST, preferred_element_type=F32,
    )
    exit_col = jnp.exp(log_col[rows - 1 : rows, :] - log_col) * keep_last
    reach_col = carried_in * jnp.exp(log_col)

    lane = lax.broadcasted_iota(jnp.int32, (1, width), 1)
    is_head = [
        jnp.logical_and(lane >= i * head_dim, lane < (i + 1) * head_dim) for i in range(GROUP)
    ]
    head_one = [m.astype(F32).astype(BF16) for m in is_head]

    def spread(columns, g):
        out = columns[:, g * GROUP + GROUP - 1 : g * GROUP + GROUP]
        for i in reversed(range(GROUP - 1)):
            out = jnp.where(is_head[i], columns[:, g * GROUP + i : g * GROUP + i + 1], out)
        return out

    def lanes(g):
        return slice(g * width, (g + 1) * width)

    def pick(square):
        out = square[(GROUP - 1) * head_dim :, :]
        for i in reversed(range(GROUP - 1)):
            out = jnp.where(is_head[i], square[i * head_dim : (i + 1) * head_dim, :], out)
        return out

    def stack(x):
        return jnp.concatenate([x * m for m in head_one], axis=0)

    def put_state(buf, g, state):
        buf[2 * g] = state[:half, :]
        buf[2 * g + 1] = state[half:, :]

    def block_diagonal(buf, g):
        state = jnp.concatenate([buf[2 * g], buf[2 * g + 1]], axis=0)
        high, low = split_pair(state)
        return stack(high), stack(low)

    for g in range(groups):
        ex = spread(exit_col, g)
        xw[:, lanes(g)] = ex
        rx = spread(reach_col, g)
        crx[:, lanes(g)] = rx * scale
        fac[2 * g] = rx[rows - 1 : rows, :]
        fac[2 * g + 1] = rx[rows - 1 : rows, :]
        high, low = split_pair(k_ref[:, lanes(g)].astype(F32) * ex)
        v = v_ref[:, lanes(g)]
        put_state(send_a, g, pick(contract(high, v, 0, 0) + contract(low, v, 0, 0)))

    pl.semaphore_wait(barrier, len(partners))

    step = half // PIECES

    def there(phase, src, dst):
        copies = []
        for j in range(PIECES):
            part = pl.ds(j * step, step)
            these = []
            for i, k in enumerate(OFFSETS):
                other = ring(k)
                copy = pltpu.make_async_remote_copy(
                    src_ref=src.at[other, part],
                    dst_ref=dst.at[z, part],
                    send_sem=there_s.at[phase, j, i],
                    recv_sem=there_r.at[phase, j, i],
                    device_id=in_line(other),
                    device_id_type=MESH,
                )
                copy.start()
                these.append(copy)
            copies.append(these)
        return copies

    fac_copies = []
    for i, k in enumerate(OFFSETS):
        other = ring(k)
        copy = pltpu.make_async_remote_copy(
            src_ref=fac.at[other],
            dst_ref=rfac.at[z],
            send_sem=fac_s.at[i],
            recv_sem=fac_r.at[i],
            device_id=in_line(other),
            device_id_type=MESH,
        )
        copy.start()
        fac_copies.append(copy)
    there_a = there(0, send_a, recv_a)
    rfac[z] = fac[z]
    recv_a[z] = send_a[z]

    for g in range(groups):
        for i in range(GROUP):
            h = g * GROUP + i
            gap = log_col[:, h : h + 1] - log_row[h : h + 1, :]
            cm[g, :, i * rows : (i + 1) * rows] = scale * jnp.exp(jnp.where(same, gap, -1e30))
        scores = contract(q_ref[:, lanes(g)], stack(k_ref[:, lanes(g)]), 1, 1)
        p = (scores * cm[g]).astype(BF16)
        probs[g] = p
        att[:, lanes(g)] = contract(p, stack(v_ref[:, lanes(g)]), 1, 0)

    def owner(phase, sign, there_copies, src, total, rtotal, rlfac, dst, come):
        order = list(range(RING)) if sign > 0 else list(reversed(range(RING)))
        line_copies = []
        for j in range(PIECES):
            part = slice(j * step, (j + 1) * step)
            for copy in there_copies[j]:
                copy.wait()
            if j == 0:
                if phase == 0:
                    for copy in fac_copies:
                        copy.wait()
                    product = rfac[0]
                    for i in range(1, RING):
                        product = product * rfac[i]
                    lfac[0] = product
            run = src[order[0], part, :]
            for i in order[1:]:
                run = src[i, part, :] + rfac[i] * run
            total[part, :] = run
            these = []
            for k in range(1, REACH + 1):
                if j == 0:
                    copy = pltpu.make_async_remote_copy(
                        src_ref=lfac.at[0],
                        dst_ref=rlfac.at[k - 1],
                        send_sem=lfac_s.at[phase, k - 1],
                        recv_sem=lfac_r.at[phase, k - 1],
                        device_id=other_line(sign * k),
                        device_id_type=MESH,
                    )
                    copy.start()
                    these.append(copy)
                copy = pltpu.make_async_remote_copy(
                    src_ref=total.at[pl.ds(j * step, step)],
                    dst_ref=rtotal.at[k - 1, pl.ds(j * step, step)],
                    send_sem=line_s.at[phase, j, k - 1],
                    recv_sem=line_r.at[phase, j, k - 1],
                    device_id=other_line(sign * k),
                    device_id_type=MESH,
                )
                copy.start()
                these.append(copy)
            line_copies.append(these)
        back_copies = []
        for j in range(PIECES):
            part = slice(j * step, (j + 1) * step)
            for copy in line_copies[j]:
                copy.wait()
            run = rtotal[REACH - 1, part, :]
            for k in reversed(range(REACH - 1)):
                run = rtotal[k, part, :] + rlfac[k] * run
            for i in order:
                dst[i, part, :] = run
                run = src[i, part, :] + rfac[i] * run
            for i, k in enumerate(OFFSETS):
                other = ring(k)
                copy = pltpu.make_async_remote_copy(
                    src_ref=dst.at[other, pl.ds(j * step, step)],
                    dst_ref=come.at[z, pl.ds(j * step, step)],
                    send_sem=back_s.at[phase, j, i],
                    recv_sem=back_r.at[phase, j, i],
                    device_id=in_line(other),
                    device_id_type=MESH,
                )
                copy.start()
                back_copies.append(copy)
        come[z] = dst[z]
        return back_copies

    for copy in owner(0, 1, there_a, recv_a, tot_a, rtot_a, rlfac_a, back_a, come_a):
        copy.wait()

    square = jnp.zeros((rows, width), F32)
    inner = jnp.zeros((rows, width), F32)
    for g in range(groups):
        high, low = block_diagonal(come_a, g)
        q = q_ref[:, lanes(g)]
        full = att[:, lanes(g)] + crx[:, lanes(g)] * (
            contract(q, high, 1, 0) + contract(q, low, 1, 0)
        )
        att[:, lanes(g)] = full
        square += full * full
        inner += og_ref[:, lanes(g)].astype(F32) * gain_ref[:, lanes(g)] * full
    square = jnp.sum(square, axis=1, keepdims=True)
    inner = jnp.sum(inner, axis=1, keepdims=True)
    first = lax.broadcasted_iota(jnp.int32, (1, 128), 1) < 64
    sums[...] = jnp.where(first, square, inner)
    copy = pltpu.make_async_remote_copy(
        src_ref=sums,
        dst_ref=rsums,
        send_sem=sum_s,
        recv_sem=sum_r,
        device_id=(place, 1 - core),
        device_id_type=MESH,
    )
    copy.start()
    copy.wait()
    both = sums[...] + rsums[...]
    inv_rms = lax.rsqrt(both[:, 0:1] / feature_count + EPSILON)
    along = inv_rms * inv_rms * inv_rms * both[:, 64:65] / feature_count

    for g in range(groups):
        a = att[:, lanes(g)]
        gg = og_ref[:, lanes(g)].astype(F32) * gain_ref[:, lanes(g)]
        gr = (gg * inv_rms - a * along).astype(BF16)
        grad[:, lanes(g)] = gr
        high, low = split_pair(q_ref[:, lanes(g)].astype(F32) * crx[:, lanes(g)])
        put_state(send_b, g, pick(contract(high, gr, 0, 0) + contract(low, gr, 0, 0)))
    there_b = there(1, send_b, recv_b)
    recv_b[z] = send_b[z]

    for g in range(groups):
        gr = grad[:, lanes(g)]
        o_ref[:, lanes(g)] = (att[:, lanes(g)] * inv_rms * gain_ref[:, lanes(g)]).astype(BF16)
        grad_scores = contract(gr, stack(v_ref[:, lanes(g)]), 1, 1)
        sg = (grad_scores * cm[g]).astype(BF16)
        high, low = block_diagonal(come_a, g)
        dq = contract(sg, stack(k_ref[:, lanes(g)]), 1, 0) + crx[:, lanes(g)] * (
            contract(gr, high, 1, 1) + contract(gr, low, 1, 1)
        )
        dq_ref[:, lanes(g)] = dq.astype(BF16)
        p = probs[g]
        tall_p = jnp.concatenate([p[:, i * rows : (i + 1) * rows] for i in range(GROUP)], axis=0)
        tall_s = jnp.concatenate([sg[:, i * rows : (i + 1) * rows] for i in range(GROUP)], axis=0)
        kpart[:, lanes(g)] = contract(tall_s, stack(q_ref[:, lanes(g)]), 0, 0)
        vpart[:, lanes(g)] = contract(tall_p, stack(gr), 0, 0)

    for copy in owner(1, -1, there_b, recv_b, tot_b, rtot_b, rlfac_b, back_b, come_b):
        copy.wait()

    for g in range(groups):
        high, low = block_diagonal(come_b, g)
        v = v_ref[:, lanes(g)]
        k = k_ref[:, lanes(g)]
        ex = xw[:, lanes(g)]
        dk_ref[:, lanes(g)] = (
            kpart[:, lanes(g)] + ex * (contract(v, high, 1, 1) + contract(v, low, 1, 1))
        ).astype(BF16)
        dv_ref[:, lanes(g)] = (
            vpart[:, lanes(g)] + ex * (contract(k, high, 1, 0) + contract(k, low, 1, 0))
        ).astype(BF16)


def solution(mesh):
    lines = mesh.shape["ctx"] // RING
    cores = mesh.shape["head"]

    def on_device(queries, keys, values, decay_log, norm_gain, out_grad, doc_lengths):
        rows, local = queries.shape
        head_dim = local // decay_log.shape[0]
        width = GROUP * head_dim
        groups = local // width
        half = head_dim // 2
        assert groups * 2 == RING and half % (8 * PIECES) == 0
        vmem = pl.BlockSpec(memory_space=pltpu.VMEM)
        state = pltpu.VMEM((RING, half, width), F32)
        total = pltpu.VMEM((half, width), F32)
        totals = pltpu.VMEM((REACH, half, width), F32)
        wide = pltpu.VMEM((rows, local), F32)
        dma = pltpu.SemaphoreType.DMA
        n = len(OFFSETS)
        out = jax.ShapeDtypeStruct((rows, local), BF16)
        return pl.pallas_call(
            functools.partial(kernel, head_dim, local * cores, lines),
            out_shape=(out, out, out, out),
            in_specs=[pl.BlockSpec(memory_space=pltpu.SMEM)] + [vmem] * 6,
            out_specs=(vmem,) * 4,
            scratch_shapes=[
                wide,
                pltpu.VMEM((rows, local), BF16),
                wide,
                wide,
                pltpu.VMEM((groups, rows, GROUP * rows), F32),
                pltpu.VMEM((groups, rows, GROUP * rows), BF16),
                wide,
                wide,
                state, state, state, state,
                state, state, state, state,
                total, totals, total, totals,
                pltpu.VMEM((RING, 1, width), F32),
                pltpu.VMEM((RING, 1, width), F32),
                pltpu.VMEM((1, 1, width), F32),
                pltpu.VMEM((REACH, 1, width), F32),
                pltpu.VMEM((REACH, 1, width), F32),
                pltpu.VMEM((rows, 128), F32),
                pltpu.VMEM((rows, 128), F32),
                dma((2, PIECES, n)), dma((2, PIECES, n)),
                dma((2, PIECES, REACH)), dma((2, PIECES, REACH)),
                dma((2, PIECES, n)), dma((2, PIECES, n)),
                dma((n,)), dma((n,)),
                dma((2, REACH)), dma((2, REACH)),
                dma, dma,
            ],
            compiler_params=pltpu.CompilerParams(collective_id=0, has_side_effects=True),
        )(
            doc_lengths,
            queries,
            keys,
            values,
            decay_log,
            norm_gain.reshape(1, local),
            out_grad,
        )

    return jax.shard_map(
        on_device,
        mesh=mesh,
        in_specs=(
            P("ctx", "head"),
            P("ctx", "head"),
            P("ctx", "head"),
            P("head", "ctx"),
            P("head"),
            P("ctx", "head"),
            P(),
        ),
        out_specs=(P("ctx", "head"),) * 4,
        check_vma=False,
    )
```

time: 1430 us -> 86.4 us (0.06)
  waiting for transfers between devices: 793 us -> 0 us
  blocking collectives: 320 us -> 0 us
  other arithmetic: 173 us -> 0 us
  local copies, waits for them, and re-layouts: 100 us -> 6.13 us
  Pallas kernels: 0 us -> 79.2 us
  between operations: 15 us -> 0.65 us
    all_gather x2 -> x0, waiting for transfers between devices: 793 us -> none  [entering(): gathered = jax.tree.map(lambda a: lax.all_gather(a, axis), part)]
    unnamed x1 -> x0, blocking collectives: 317 us -> none
    add x128 -> x0, other arithmetic: 166 us -> none  [the longest x127 166 us: combine(): later_pair[0][:, None, None] * earlier[1] + later_pair[1]]
    mul x127 -> x0, local copies, waits for them, and re-layouts: 87.3 us -> none  [combine(): later_pair[0][:, None, None] * earlier[1] + later_pair[1]]
    pallas_call x0 -> x1, Pallas kernels: none -> 79.2 us  [on_device(): pl.pallas_call(functools.partial(kernel, head_dim, local * cores, lines),...]
  transfers between devices with their start and end apart: 2 -> 0, of which waited for: 2 -> 0; matrix products, arithmetic and copies ran while one was open for 1% -> 0% of each run, Pallas kernels for 0% -> 0%
where the time goes in v1:
time: 86.4 us; the launch traced here: 86 us
  Pallas kernels  79.2 us (92%)
  local copies, waits for them, and re-layouts  6.13 us (7%)
    pallas_call x1, Pallas kernels, on_device(): pl.pallas_call(functools.partial(kernel, head_dim, local * cores, lines),...  79.2 us
    unnamed x10, local copies, waits for them, and re-layouts  4.84 us

profile of v1, /device:TPU:1, one launch (start us, length us, event | category | flops | bytes accessed | tf_op | source)
XLA Modules:
  0.0 86.0 jit_solution(3541836421662180030)
XLA Ops:
  0.6 1.3 %reshape.11.gain_ref = f32[1,1536]{1,0:T(1,128)} reshape(f32[1536]{0:T(1024)} %param.11) | data formatting | bytes 12288 | tf_op jit(solution)/shard_map/reshape | solution.py:441
  1.9 79.2 %shard_map.102 = (bf16[128,1536]{1,0:T(8,128)(2,1)}, bf16[128,1536]{1,0:T(8,128)(2,1)}, bf16[128,1536]{1,0:T(8,128)(2,1)}, bf16[128,1536]{1,0:T(8,128)(2,1)}) custom-call(s32[16]{0:T(128)} %docs.1, bf16[128,1536]{1,0:T(8,128)(2,1)} %q_ref.1, bf16[128,1536]{1,0:T(8,128)(2,1)} %k_ref.1, bf16[128,1536]{1,0:T(8,128)(2,1)} %v_ref.1, f32[16,128]{1,0:T(8,128)} %decay_ref.1, ...), custom_call_target="tpu_custom_call" | custom-call | tf_op jit(solution)/shard_map/pallas_call | solution.py:403
  81.2 0.0 copy-start.2
  81.2 1.8 %copy.15 = bf16[128,1536]{1,0:T(8,128)(2,1)} copy(bf16[128,1536]{1,0:T(8,128)(2,1)} %get-tuple-element.8) | data formatting | bytes 786432
  83.0 0.0 copy-done.2
  83.0 0.0 copy-start.1
  83.0 0.7 copy.16
  83.7 0.4 copy-done.1
  84.1 0.0 copy-start
  84.1 0.7 copy.17
  84.9 0.4 copy-done
  85.3 0.7 copy.18
Async XLA Ops:
  81.2 1.8 %copy-start.2 = (bf16[128,1536]{1,0:T(8,128)(2,1)S(1)}, bf16[128,1536]{1,0:T(8,128)(2,1)}, u32[]{:S(2)}) copy-start(bf16[128,1536]{1,0:T(8,128)(2,1)} %get-tuple-element.9) | copy-start | bytes 1179652
  83.0 1.1 %copy-start.1 = (bf16[128,1536]{1,0:T(8,128)(2,1)S(1)}, bf16[128,1536]{1,0:T(8,128)(2,1)}, u32[]{:S(2)}) copy-start(bf16[128,1536]{1,0:T(8,128)(2,1)} %get-tuple-element.10) | copy-start | bytes 1179652
  84.1 1.1 %copy-start = (bf16[128,1536]{1,0:T(8,128)(2,1)S(1)}, bf16[128,1536]{1,0:T(8,128)(2,1)}, u32[]{:S(2)}) copy-start(bf16[128,1536]{1,0:T(8,128)(2,1)} %get-tuple-element.11) | copy-start | bytes 1179652

commit v2 on v1

--- a/solution.py
+++ b/solution.py
@@ -17,16 +17,12 @@
 REACH = 4
 GROUP = 4
 OFFSETS = (1, -1, 2, -2, 3, -3, 4)
-PIECES = 2
+PIECES = 3
+LAG = 1
 
 
 def contract(a, b, ca, cb):
     return lax.dot_general(a, b, (((ca,), (cb,)), ((), ())), preferred_element_type=F32)
-
-
-def split_pair(x):
-    high = x.astype(BF16)
-    return high, (x - high.astype(F32)).astype(BF16)
 
 
 def kernel(
@@ -158,6 +154,12 @@
     def lanes(g):
         return slice(g * width, (g + 1) * width)
 
+    def gain(g):
+        tiles = width // 128
+        return jnp.concatenate(
+            [gain_ref[i : i + 1, :] for i in range(g * tiles, (g + 1) * tiles)], axis=1
+        )
+
     def pick(square):
         out = square[(GROUP - 1) * head_dim :, :]
         for i in reversed(range(GROUP - 1)):
@@ -173,8 +175,7 @@
 
     def block_diagonal(buf, g):
         state = jnp.concatenate([buf[2 * g], buf[2 * g + 1]], axis=0)
-        high, low = split_pair(state)
-        return stack(high), stack(low)
+        return stack(state.astype(BF16))
 
     for g in range(groups):
         ex = spread(exit_col, g)
@@ -183,9 +184,8 @@
         crx[:, lanes(g)] = rx * scale
         fac[2 * g] = rx[rows - 1 : rows, :]
         fac[2 * g + 1] = rx[rows - 1 : rows, :]
-        high, low = split_pair(k_ref[:, lanes(g)].astype(F32) * ex)
-        v = v_ref[:, lanes(g)]
-        put_state(send_a, g, pick(contract(high, v, 0, 0) + contract(low, v, 0, 0)))
+        weighted = (k_ref[:, lanes(g)].astype(F32) * ex).astype(BF16)
+        put_state(send_a, g, pick(contract(weighted, v_ref[:, lanes(g)], 0, 0)))
 
     pl.semaphore_wait(barrier, len(partners))
 
@@ -241,18 +241,19 @@
     def owner(phase, sign, there_copies, src, total, rtotal, rlfac, dst, come):
         order = list(range(RING)) if sign > 0 else list(reversed(range(RING)))
         line_copies = []
-        for j in range(PIECES):
+        back_copies = []
+
+        def arrive(j):
             part = slice(j * step, (j + 1) * step)
+            if phase == 0 and j == 0:
+                for copy in fac_copies:
+                    copy.wait_recv()
+                product = rfac[0]
+                for i in range(1, RING):
+                    product = product * rfac[i]
+                lfac[0] = product
             for copy in there_copies[j]:
-                copy.wait()
-            if j == 0:
-                if phase == 0:
-                    for copy in fac_copies:
-                        copy.wait()
-                    product = rfac[0]
-                    for i in range(1, RING):
-                        product = product * rfac[i]
-                    lfac[0] = product
+                copy.wait_recv()
             run = src[order[0], part, :]
             for i in order[1:]:
                 run = src[i, part, :] + rfac[i] * run
@@ -281,11 +282,11 @@
                 copy.start()
                 these.append(copy)
             line_copies.append(these)
-        back_copies = []
-        for j in range(PIECES):
+
+        def send_back(j):
             part = slice(j * step, (j + 1) * step)
             for copy in line_copies[j]:
-                copy.wait()
+                copy.wait_recv()
             run = rtotal[REACH - 1, part, :]
             for k in reversed(range(REACH - 1)):
                 run = rtotal[k, part, :] + rlfac[k] * run
@@ -304,23 +305,29 @@
                 )
                 copy.start()
                 back_copies.append(copy)
+
+        for tick in range(PIECES + LAG):
+            if tick < PIECES:
+                arrive(tick)
+            if tick >= LAG:
+                send_back(tick - LAG)
         come[z] = dst[z]
-        return back_copies
-
-    for copy in owner(0, 1, there_a, recv_a, tot_a, rtot_a, rlfac_a, back_a, come_a):
-        copy.wait()
+        for copy in back_copies:
+            copy.wait_recv()
+        sent = [copy for these in there_copies + line_copies for copy in these] + back_copies
+        return sent + (fac_copies if phase == 0 else [])
+
+    sent = owner(0, 1, there_a, recv_a, tot_a, rtot_a, rlfac_a, back_a, come_a)
 
     square = jnp.zeros((rows, width), F32)
     inner = jnp.zeros((rows, width), F32)
     for g in range(groups):
-        high, low = block_diagonal(come_a, g)
-        q = q_ref[:, lanes(g)]
-        full = att[:, lanes(g)] + crx[:, lanes(g)] * (
-            contract(q, high, 1, 0) + contract(q, low, 1, 0)
+        full = att[:, lanes(g)] + crx[:, lanes(g)] * contract(
+            q_ref[:, lanes(g)], block_diagonal(come_a, g), 1, 0
         )
         att[:, lanes(g)] = full
         square += full * full
-        inner += og_ref[:, lanes(g)].astype(F32) * gain_ref[:, lanes(g)] * full
+        inner += og_ref[:, lanes(g)].astype(F32) * gain(g) * full
     square = jnp.sum(square, axis=1, keepdims=True)
     inner = jnp.sum(inner, axis=1, keepdims=True)
     first = lax.broadcasted_iota(jnp.int32, (1, 128), 1) < 64
@@ -341,22 +348,21 @@
 
     for g in range(groups):
         a = att[:, lanes(g)]
-        gg = og_ref[:, lanes(g)].astype(F32) * gain_ref[:, lanes(g)]
+        gg = og_ref[:, lanes(g)].astype(F32) * gain(g)
         gr = (gg * inv_rms - a * along).astype(BF16)
         grad[:, lanes(g)] = gr
-        high, low = split_pair(q_ref[:, lanes(g)].astype(F32) * crx[:, lanes(g)])
-        put_state(send_b, g, pick(contract(high, gr, 0, 0) + contract(low, gr, 0, 0)))
+        reached = (q_ref[:, lanes(g)].astype(F32) * crx[:, lanes(g)]).astype(BF16)
+        put_state(send_b, g, pick(contract(reached, gr, 0, 0)))
     there_b = there(1, send_b, recv_b)
     recv_b[z] = send_b[z]
 
     for g in range(groups):
         gr = grad[:, lanes(g)]
-        o_ref[:, lanes(g)] = (att[:, lanes(g)] * inv_rms * gain_ref[:, lanes(g)]).astype(BF16)
+        o_ref[:, lanes(g)] = (att[:, lanes(g)] * inv_rms * gain(g)).astype(BF16)
         grad_scores = contract(gr, stack(v_ref[:, lanes(g)]), 1, 1)
         sg = (grad_scores * cm[g]).astype(BF16)
-        high, low = block_diagonal(come_a, g)
-        dq = contract(sg, stack(k_ref[:, lanes(g)]), 1, 0) + crx[:, lanes(g)] * (
-            contract(gr, high, 1, 1) + contract(gr, low, 1, 1)
+        dq = contract(sg, stack(k_ref[:, lanes(g)]), 1, 0) + crx[:, lanes(g)] * contract(
+            gr, block_diagonal(come_a, g), 1, 1
         )
         dq_ref[:, lanes(g)] = dq.astype(BF16)
         p = probs[g]
@@ -365,20 +371,29 @@
         kpart[:, lanes(g)] = contract(tall_s, stack(q_ref[:, lanes(g)]), 0, 0)
         vpart[:, lanes(g)] = contract(tall_p, stack(gr), 0, 0)
 
-    for copy in owner(1, -1, there_b, recv_b, tot_b, rtot_b, rlfac_b, back_b, come_b):
-        copy.wait()
-
-    for g in range(groups):
-        high, low = block_diagonal(come_b, g)
-        v = v_ref[:, lanes(g)]
-        k = k_ref[:, lanes(g)]
+    sent += owner(1, -1, there_b, recv_b, tot_b, rtot_b, rlfac_b, back_b, come_b)
+
+    for g in range(groups):
+        later = block_diagonal(come_b, g)
         ex = xw[:, lanes(g)]
         dk_ref[:, lanes(g)] = (
-            kpart[:, lanes(g)] + ex * (contract(v, high, 1, 1) + contract(v, low, 1, 1))
+            kpart[:, lanes(g)] + ex * contract(v_ref[:, lanes(g)], later, 1, 1)
         ).astype(BF16)
         dv_ref[:, lanes(g)] = (
-            vpart[:, lanes(g)] + ex * (contract(k, high, 1, 0) + contract(k, low, 1, 0))
+            vpart[:, lanes(g)] + ex * contract(k_ref[:, lanes(g)], later, 1, 0)
         ).astype(BF16)
+    for copy in sent:
+        copy.wait_send()
+
+
+def deliver(*refs):
+    n = len(refs) // 2
+    sems = refs[-1]
+    copies = [pltpu.make_async_copy(refs[i], refs[n + i], sems.at[i]) for i in range(n)]
+    for copy in copies:
+        copy.start()
+    for copy in copies:
+        copy.wait()
 
 
 def solution(mesh):
@@ -399,8 +414,8 @@
         wide = pltpu.VMEM((rows, local), F32)
         dma = pltpu.SemaphoreType.DMA
         n = len(OFFSETS)
-        out = jax.ShapeDtypeStruct((rows, local), BF16)
-        return pl.pallas_call(
+        out = pltpu.VMEM((rows, local), BF16)
+        results = pl.pallas_call(
             functools.partial(kernel, head_dim, local * cores, lines),
             out_shape=(out, out, out, out),
             in_specs=[pl.BlockSpec(memory_space=pltpu.SMEM)] + [vmem] * 6,
@@ -438,9 +453,16 @@
             keys,
             values,
             decay_log,
-            norm_gain.reshape(1, local),
+            norm_gain.reshape(local // 128, 128),
             out_grad,
         )
+        return pl.pallas_call(
+            deliver,
+            out_shape=(jax.ShapeDtypeStruct((rows, local), BF16),) * 4,
+            in_specs=[vmem] * 4,
+            out_specs=(pl.BlockSpec(memory_space=pl.ANY),) * 4,
+            scratch_shapes=[dma((4,))],
+        )(*[pltpu.with_memory_space_constraint(r, pltpu.VMEM) for r in results])
 
     return jax.shard_map(
         on_device,

time: 86.4 us -> 76 us (0.88)
  local copies, waits for them, and re-layouts: 6.13 us -> 0 us
  Pallas kernels: 79.2 us -> 74.7 us
    pallas_call x1, Pallas kernels: 79.2 us -> 73.5 us  [on_device(): pl.pallas_call(functools.partial(kernel, head_dim, local * cores, lines),...]
    unnamed x10 -> x0, local copies, waits for them, and re-layouts: 4.84 us -> none
    reshape x1 -> x0, local copies, waits for them, and re-layouts: 1.3 us -> none  [on_device(): norm_gain.reshape(1, local)]
    pallas_call x0 -> x1, Pallas kernels: none -> 1.17 us  [on_device(): pl.pallas_call(deliver, out_shape=(jax.ShapeDtypeStruct((rows, local), BF...]
where the time goes in v2:
time: 76 us; the launch traced here: 75.3 us
  Pallas kernels  74.7 us (98%)
    pallas_call x1, Pallas kernels, on_device(): pl.pallas_call(functools.partial(kernel, head_dim, local * cores, lines),...  73.5 us

profile of v2, /device:TPU:1, one launch (start us, length us, event | category | flops | bytes accessed | tf_op | source)
XLA Modules:
  0.0 75.3 jit_solution(17068462488304232451)
XLA Ops:
  0.6 73.5 %shard_map.102 = (bf16[128,1536]{1,0:T(8,128)(2,1)S(1)}, bf16[128,1536]{1,0:T(8,128)(2,1)S(1)}, bf16[128,1536]{1,0:T(8,128)(2,1)S(1)}, bf16[128,1536]{1,0:T(8,128)(2,1)S(1)}) custom-call(s32[16]{0:T(128)} %docs.1, bf16[128,1536]{1,0:T(8,128)(2,1)} %q_ref.1, bf16[128,1536]{1,0:T(8,128)(2,1)} %k_ref.1, bf16[128,1536]{1,0:T(8,128)(2,1)} %v_ref.1, ...), custom_call_target="tpu_custom_call" | custom-call | tf_op jit(solution)/shard_map/pallas_call | solution.py:418
  74.1 1.2 %shard_map.103 = (bf16[128,1536]{1,0:T(8,128)(2,1)}, bf16[128,1536]{1,0:T(8,128)(2,1)}, bf16[128,1536]{1,0:T(8,128)(2,1)}, bf16[128,1536]{1,0:T(8,128)(2,1)}) custom-call(bf16[128,1536]{1,0:T(8,128)(2,1)S(1)} %get-tuple-element.8.refs_0_, bf16[128,1536]{1,0:T(8,128)(2,1)S(1)} %get-tuple-element.9.refs_1_, bf16[128,1536]{1,0:T(8,128)(2,1)S(1)} %get-tuple-element.10.refs_2_, ...), custom_call_target="tpu_custom_call" | custom-call | tf_op jit(solution)/shard_map/pallas_call | solution.py:459

commit v3 on v2

--- a/solution.py
+++ b/solution.py
@@ -16,7 +16,7 @@
 RING = 8
 REACH = 4
 GROUP = 4
-OFFSETS = (1, -1, 2, -2, 3, -3, 4)
+OFFSETS = (4, 3, -3, 2, -2, 1, -1)
 PIECES = 3
 LAG = 1
 

time: 76 us -> 74.3 us (0.978)
  Pallas kernels: 74.7 us -> 73.5 us
    pallas_call x1, Pallas kernels: 73.5 us -> 72.4 us  [on_device(): pl.pallas_call(functools.partial(kernel, head_dim, local * cores, lines),...]
where the time goes in v3:
time: 74.3 us; the launch traced here: 74.2 us
  Pallas kernels  73.5 us (99%)
    pallas_call x1, Pallas kernels, on_device(): pl.pallas_call(functools.partial(kernel, head_dim, local * cores, lines),...  72.4 us

profile of v3, /device:TPU:1, one launch (start us, length us, event | category | flops | bytes accessed | tf_op | source)
XLA Modules:
  0.0 74.2 jit_solution(4409889082359567127)
XLA Ops:
  0.6 72.4 %shard_map.102 = (bf16[128,1536]{1,0:T(8,128)(2,1)S(1)}, bf16[128,1536]{1,0:T(8,128)(2,1)S(1)}, bf16[128,1536]{1,0:T(8,128)(2,1)S(1)}, bf16[128,1536]{1,0:T(8,128)(2,1)S(1)}) custom-call(s32[16]{0:T(128)} %docs.1, bf16[128,1536]{1,0:T(8,128)(2,1)} %q_ref.1, bf16[128,1536]{1,0:T(8,128)(2,1)} %k_ref.1, bf16[128,1536]{1,0:T(8,128)(2,1)} %v_ref.1, ...), custom_call_target="tpu_custom_call" | custom-call | tf_op jit(solution)/shard_map/pallas_call | solution.py:418
  73.0 1.2 %shard_map.103 = (bf16[128,1536]{1,0:T(8,128)(2,1)}, bf16[128,1536]{1,0:T(8,128)(2,1)}, bf16[128,1536]{1,0:T(8,128)(2,1)}, bf16[128,1536]{1,0:T(8,128)(2,1)}) custom-call(bf16[128,1536]{1,0:T(8,128)(2,1)S(1)} %get-tuple-element.8.refs_0_, bf16[128,1536]{1,0:T(8,128)(2,1)S(1)} %get-tuple-element.9.refs_1_, bf16[128,1536]{1,0:T(8,128)(2,1)S(1)} %get-tuple-element.10.refs_2_, ...), custom_call_target="tpu_custom_call" | custom-call | tf_op jit(solution)/shard_map/pallas_call | solution.py:459

commit v4 on v3

--- a/solution.py
+++ b/solution.py
@@ -16,6 +16,7 @@
 RING = 8
 REACH = 4
 GROUP = 4
+LINE_ORDER = (2, 3, 1, 4)
 OFFSETS = (4, 3, -3, 2, -2, 1, -1)
 PIECES = 3
 LAG = 1
@@ -259,7 +260,7 @@
                 run = src[i, part, :] + rfac[i] * run
             total[part, :] = run
             these = []
-            for k in range(1, REACH + 1):
+            for k in LINE_ORDER:
                 if j == 0:
                     copy = pltpu.make_async_remote_copy(
                         src_ref=lfac.at[0],

time: 74.3 us -> 74.5 us (level)
  no operation moved by 1% of the time
where the time goes in v4:
time: 74.5 us; the launch traced here: 74.4 us
  Pallas kernels  73.8 us (99%)
    pallas_call x1, Pallas kernels, on_device(): pl.pallas_call(functools.partial(kernel, head_dim, local * cores, lines),...  72.6 us

profile of v4, /device:TPU:1, one launch (start us, length us, event | category | flops | bytes accessed | tf_op | source)
XLA Modules:
  0.0 74.4 jit_solution(3585252851336633005)
XLA Ops:
  0.6 72.6 %shard_map.102 = (bf16[128,1536]{1,0:T(8,128)(2,1)S(1)}, bf16[128,1536]{1,0:T(8,128)(2,1)S(1)}, bf16[128,1536]{1,0:T(8,128)(2,1)S(1)}, bf16[128,1536]{1,0:T(8,128)(2,1)S(1)}) custom-call(s32[16]{0:T(128)} %docs.1, bf16[128,1536]{1,0:T(8,128)(2,1)} %q_ref.1, bf16[128,1536]{1,0:T(8,128)(2,1)} %k_ref.1, bf16[128,1536]{1,0:T(8,128)(2,1)} %v_ref.1, ...), custom_call_target="tpu_custom_call" | custom-call | tf_op jit(solution)/shard_map/pallas_call | solution.py:419
  73.2 1.2 %shard_map.103 = (bf16[128,1536]{1,0:T(8,128)(2,1)}, bf16[128,1536]{1,0:T(8,128)(2,1)}, bf16[128,1536]{1,0:T(8,128)(2,1)}, bf16[128,1536]{1,0:T(8,128)(2,1)}) custom-call(bf16[128,1536]{1,0:T(8,128)(2,1)S(1)} %get-tuple-element.8.refs_0_, bf16[128,1536]{1,0:T(8,128)(2,1)S(1)} %get-tuple-element.9.refs_1_, bf16[128,1536]{1,0:T(8,128)(2,1)S(1)} %get-tuple-element.10.refs_2_, ...), custom_call_target="tpu_custom_call" | custom-call | tf_op jit(solution)/shard_map/pallas_call | solution.py:460
